TPU v7x, 32 devices: a whole 2x2x4 slice. The times are simulated.
32 devices in a mesh: dp: 4 (over z), seq: 8 (over y, x, core).
Axes of the slice: x: 2, y: 2, z: 4, core: 2. Of those that a mesh axis runs over, the one named last changes fastest.
Arguments:
- saved_codes: bfloat16 [4, 1024, 1536], P('dp', 'seq'), may hold values from -6 to 6
- code_scales: float32 [4, 12, 1024], P('dp', None, 'seq'), may hold values from 0.25 to 4
- lengths: int32 [4], replicated, may hold values from 128 to 1024, as said below
- in_weight: bfloat16 [3072, 1536], P('dp'), may hold values from -0.15625 to 0.15625
- conv_kernel: float32 [31, 1536], replicated, may hold values from -1 to 1
- bn_gain: float32 [1536], replicated, may hold values from 0.1 to 1.9
- bn_shift: float32 [1536], replicated, may hold values from -3 to 3
- out_grad: bfloat16 [4, 1024, 1536], P('dp', 'seq'), may hold values from -6 to 6
Outputs:
- in_grad: bfloat16 [4, 1024, 1536], P('dp', 'seq')
- weight_grad: float32 [3072, 1536], P('dp')
- kernel_grad: float32 [31, 1536], replicated
- gain_grad: float32 [1536], replicated
- shift_grad: float32 [1536], replicated
Inputs may be any that keep to these rules, and one draw needn't show every extreme that they name: `lengths`: at least one recording has exactly 1024 valid frames.
All inputs are finite; a program needn't handle non-finite values.
Results may differ from a plain program's by a relative error of at most 0.0067.
Values may be sent and summed in bfloat16 or wider, within the bound.
A program may use at most 128 MiB of HBM per device.

v0:
```python
import jax
import jax.numpy as jnp
from jax import lax
from jax.sharding import PartitionSpec as P

EPS = 1e-05


def padded_2(cells, sides, width):
    for axis, dim in sides:
        count = lax.axis_size(axis)
        ends = count - 1
        head = lax.slice_in_dim(cells, 0, width, axis=dim)
        tail = lax.slice_in_dim(cells, cells.shape[dim] - width, cells.shape[dim], axis=dim)
        cells = jnp.concatenate(
            [
                lax.ppermute(tail, axis, [(i, (i + 1) % count) for i in range(ends)]),
                cells,
                lax.ppermute(head, axis, [((i + 1) % count, i) for i in range(ends)]),
            ],
            axis=dim,
        )
    return cells


def restore(quantized, scales):
    per_channel = jnp.repeat(scales.T, 128, axis=1)
    return (quantized.astype(jnp.float32) * per_channel).astype(jnp.bfloat16)


def depthwise(padded, kernel, frames):
    running = jnp.zeros((frames, padded.shape[1]), jnp.float32)
    for offset in range(kernel.shape[0]):
        running = running + kernel[offset] * padded[offset : offset + frames].astype(jnp.float32)
    return running


def per_device(
    saved_codes, code_scales, lengths, in_weight, conv_kernel, bn_gain, bn_shift, out_grad
):
    frames = saved_codes.shape[1]
    feature_width = saved_codes.shape[2]
    tap_count = conv_kernel.shape[0]
    half_span = (tap_count - 1) // 2
    groups = lengths.shape[0]
    group_at = lax.axis_index("dp")
    length = jnp.sum(jnp.where(jnp.arange(groups, dtype=jnp.int32) == group_at, lengths, 0))
    counted = jnp.sum(lengths).astype(jnp.float32)
    first_frame = lax.axis_index("seq") * frames
    valid_mask = (first_frame + jnp.arange(frames, dtype=jnp.int32) < length).astype(jnp.float32)[
        :, None
    ]
    restored = restore(saved_codes[0], code_scales[0])
    weights = lax.all_gather(in_weight, "dp", axis=0, tiled=True)
    pre_act = lax.dot_general(
        restored, weights, (((1,), (1,)), ((), ())), preferred_element_type=jnp.float32
    )
    linear = pre_act[:, :feature_width]
    gate_part = jax.nn.sigmoid(pre_act[:, feature_width:])
    gated = (linear * gate_part * valid_mask).astype(jnp.bfloat16)
    gated_pad = padded_2(gated, (("seq", 0),), half_span)
    conv_out = depthwise(gated_pad, conv_kernel, frames)
    mean_value = lax.psum(jnp.sum(conv_out * valid_mask, axis=0), ("dp", "seq")) / counted
    centered = (conv_out - mean_value) * valid_mask
    variance = lax.psum(jnp.sum(centered * centered, axis=0), ("dp", "seq")) / counted
    inverse = lax.rsqrt(variance + EPS)
    normed = (conv_out - mean_value) * inverse
    shaped = bn_gain * normed + bn_shift
    smooth = jax.nn.sigmoid(shaped)
    grad_shaped = (
        out_grad[0].astype(jnp.float32) * valid_mask * smooth * (1.0 + shaped * (1.0 - smooth))
    )
    shift_grad, gain_grad = lax.psum(
        (jnp.sum(grad_shaped, axis=0), jnp.sum(grad_shaped * normed, axis=0)), ("dp", "seq")
    )
    grad_conv = (
        bn_gain * inverse * (grad_shaped - (shift_grad + normed * gain_grad) / counted) * valid_mask
    )
    kernel_part = jnp.stack(
        [
            jnp.sum(grad_conv * gated_pad[offset : offset + frames].astype(jnp.float32), axis=0)
            for offset in range(tap_count)
        ]
    )
    kernel_grad = lax.psum(kernel_part, ("dp", "seq"))
    grad_pad = padded_2(grad_conv, (("seq", 0),), half_span)
    grad_gated = depthwise(grad_pad, conv_kernel[::-1], frames) * valid_mask
    grad_pre = jnp.concatenate(
        [grad_gated * gate_part, grad_gated * linear * gate_part * (1.0 - gate_part)], axis=1
    ).astype(jnp.bfloat16)
    in_grad = jnp.dot(grad_pre, weights, preferred_element_type=jnp.float32)
    own_columns = lax.all_to_all(grad_pre[None], "dp", split_axis=2, concat_axis=0, tiled=True)
    local_rows = lax.dot_general(
        own_columns,
        lax.all_gather(restored[None], "dp", axis=0, tiled=True),
        (((0, 1), (0, 1)), ((), ())),
        preferred_element_type=jnp.float32,
    )
    weight_grad = lax.psum(local_rows, "seq")
    return (in_grad.astype(jnp.bfloat16)[None], weight_grad, kernel_grad, gain_grad, shift_grad)


def solution(mesh):
    in_specs = (
        P("dp", "seq", None),
        P("dp", None, "seq"),
        P(),
        P("dp", None),
        P(),
        P(),
        P(),
        P("dp", "seq", None),
    )
    out_specs = (P("dp", "seq", None), P("dp", None), P(), P(), P())
    return jax.shard_map(
        per_device, mesh=mesh, in_specs=in_specs, out_specs=out_specs, check_vma=False
    )
```

profile of v0, /device:TPU:0, one launch (start us, length us, event | category | flops | bytes accessed | tf_op | source)
XLA Modules:
  0.0 607.7 jit_solution(5439914261031607796)
XLA Ops:
  10.8 168.2 %all-gather.3.cloned.1.call-done = bf16[3072,1536]{1,0:T(8,128)(2,1)} async-done(((bf16[768,1536]{1,0:T(8,128)(2,1)}), bf16[3072,1536]{1,0:T(8,128)(2,1)}) %all-gather.3.cloned.1.call-update) | async-done | bytes 9437200 | tf_op jit(solution)/shard_map/all_gather | solution.py:54
  179.1 6.9 %fusion.199 = f32[128,3072]{1,0:T(8,128)S(1)} fusion(bf16[128,1536]{0,1:T(8,128)(2,1)S(1)} %fusion.150, bf16[3072,1536]{1,0:T(8,128)(2,1)} %all-gather.3.cloned.1.call-done), kind=kOutput, calls=%fused_computation.398 | convolution fusion | flops 1207959552 | bytes 11403264 | tf_op jit(solution)/shard_map/dot_general | solution.py:55
  186.2 1.4 collective-permute-start.1
  187.7 3.0 collective-permute-start
  192.3 5.1 multiply_reduce_fusion.2
  197.4 40.2 %psum.42 = f32[1536]{0:T(1024)S(1)} all-reduce(f32[1536]{0:T(1024)S(1)} %get-tuple-element.78), channel_id=1, replica_groups=mesh['dp'=4,'seq'=8] {'dp','seq'}, use_global_device_ids=true, to_apply=%region_2.3 | all-reduce | flops 1536 | bytes 12288 | tf_op jit(solution)/shard_map/psum | solution.py:63
  237.8 42.5 %psum.43 = f32[1536]{0:T(1024)S(1)} all-reduce(f32[1536]{0:T(1024)S(1)} %multiply_reduce_fusion.1), channel_id=1, replica_groups=mesh['dp'=4,'seq'=8] {'dp','seq'}, use_global_device_ids=true, to_apply=%region_5.6 | all-reduce | flops 1536 | bytes 12288 | tf_op jit(solution)/shard_map/psum | solution.py:65
  280.3 1.3 fusion.195
  281.6 1.2 fusion.192
  282.9 38.3 %all-reduce = (f32[1536]{0:T(1024)}, f32[1536]{0:T(1024)}) all-reduce(f32[1536]{0:T(1024)S(1)} %get-tuple-element.36, f32[1536]{0:T(1024)S(1)} %get-tuple-element.35), channel_id=1, replica_groups=mesh['dp'=4,'seq'=8] {'dp','seq'}, use_global_device_ids=true, to_apply=%region_9.10 | all-reduce | flops 3072 | bytes 24576 | tf_op jit(solution)/shard_map/psum | solution.py:73
  321.1 3.8 fusion.148
  324.9 1.3 collective-permute-start.3
  326.2 3.2 collective-permute-start.2
  331.5 5.4 multiply_convert_fusion.1
  338.0 1.9 copy.22
  340.5 17.0 %reduce.62 = bf16[3072,128]{1,0:T(8,128)(2,1)S(1)} reduce(bf16[3072,1,128]{2,1,0:T(2,128)(2,1)S(1)} %bitcast.43, bf16[]{:T(256)} %broadcast.68), dimensions={1}, to_apply=%bitcast.34.reduce_sub_computation | reduce | bytes 1572866
  358.4 3.5 all-to-all-start
  365.3 2.8 stack.127
  368.3 18.3 %all-to-all-done = bf16[4,2,49152]{2,1,0:T(2,128)(2,1)S(1)} async-done(((bf16[4,2,49152]{2,1,0:T(2,128)(2,1)}), bf16[4,2,49152]{2,1,0:T(2,128)(2,1)S(1)}, u32[]{:S(2)}, u32[]{:S(2)}) %all-to-all-start) | async-done | bytes 786464 | tf_op jit(solution)/shard_map/all_to_all | solution.py:92
  387.5 4.4 convolution_bitcast_fusion
  393.0 5.8 fusion
  398.9 105.5 %all-reduce.6.cloned.1.call-done = f32[31,1536]{1,0:T(8,128)} async-done(((f32[31,1536]{1,0:T(8,128)}), f32[31,1536]{1,0:T(8,128)}) %all-reduce.6.cloned.1.call-update) | async-done | bytes 190480 | tf_op jit(solution)/shard_map/psum | solution.py:85
  504.4 91.3 %all-reduce.4.cloned.1.call-done = f32[768,1536]{1,0:T(8,128)} async-done(((f32[768,1536]{1,0:T(8,128)}), f32[768,1536]{1,0:T(8,128)}) %all-reduce.4.cloned.1.call-update) | async-done | bytes 4718608 | tf_op jit(solution)/shard_map/psum | solution.py:99
  595.7 4.8 copy.30
  (150 shorter events, 15.3 us)
Async XLA Ops:
  7.2 171.9 %all-gather.3.cloned.1.call-start = ((), (), s32[]{:S(2)}) async-start(), calls=%async_computation.1 | async-start | bytes 11796480 | tf_op jit(solution)/shard_map/all_gather | solution.py:54
  7.9 379.6 %all-gather.5.cloned.1.call-start = ((), (), s32[]{:S(2)}) async-start(), calls=%async_computation.2 | async-start | bytes 1966080 | tf_op jit(solution)/shard_map/all_gather | solution.py:95
  8.4 170.7 %copy-start = (bf16[1,128,1536]{1,2,0:T(8,128)(2,1)}, bf16[1,128,1536]{1,2,0:T(8,128)(2,1)S(1)}, u32[]{:S(2)}) copy-start(bf16[1,128,1536]{1,2,0:T(8,128)(2,1)S(1)} %copy.21) | copy-start | bytes 1179652
  9.8 176.1 %copy-start.37 = (f32[128]{0:T(128)}, f32[128]{0:T(128)S(1)}, u32[]{:S(2)}) copy-start(f32[128]{0:T(128)S(1)} %compare_convert_fusion) | copy-start | bytes 1540
  10.8 181.5 %copy-start.13 = (f32[1536]{0:T(1024)}, f32[1536]{0:T(1024)S(1)}, u32[]{:S(2)}) copy-start(f32[1536]{0:T(1024)S(1)} %get-tuple-element.38) | copy-start | bytes 18436
  10.8 181.5 %copy-start.15 = (f32[1536]{0:T(1024)}, f32[1536]{0:T(1024)S(1)}, u32[]{:S(2)}) copy-start(f32[1536]{0:T(1024)S(1)} %get-tuple-element.39) | copy-start | bytes 18436
  10.8 181.5 %copy-start.16 = (f32[1536]{0:T(1024)}, f32[1536]{0:T(1024)S(1)}, u32[]{:S(2)}) copy-start(f32[1536]{0:T(1024)S(1)} %get-tuple-element.40) | copy-start | bytes 18436
  10.8 181.5 %copy-start.17 = (f32[1536]{0:T(1024)}, f32[1536]{0:T(1024)S(1)}, u32[]{:S(2)}) copy-start(f32[1536]{0:T(1024)S(1)} %get-tuple-element.41) | copy-start | bytes 18436
  10.8 181.5 %copy-start.18 = (f32[1536]{0:T(1024)}, f32[1536]{0:T(1024)S(1)}, u32[]{:S(2)}) copy-start(f32[1536]{0:T(1024)S(1)} %get-tuple-element.42) | copy-start | bytes 18436
  10.8 181.5 %copy-start.19 = (f32[1536]{0:T(1024)}, f32[1536]{0:T(1024)S(1)}, u32[]{:S(2)}) copy-start(f32[1536]{0:T(1024)S(1)} %get-tuple-element.43) | copy-start | bytes 18436
  10.8 181.5 %copy-start.20 = (f32[1536]{0:T(1024)}, f32[1536]{0:T(1024)S(1)}, u32[]{:S(2)}) copy-start(f32[1536]{0:T(1024)S(1)} %get-tuple-element.44) | copy-start | bytes 18436
  10.8 181.5 %copy-start.21 = (f32[1536]{0:T(1024)}, f32[1536]{0:T(1024)S(1)}, u32[]{:S(2)}) copy-start(f32[1536]{0:T(1024)S(1)} %get-tuple-element.45) | copy-start | bytes 18436
  10.8 181.5 %copy-start.22 = (f32[1536]{0:T(1024)}, f32[1536]{0:T(1024)S(1)}, u32[]{:S(2)}) copy-start(f32[1536]{0:T(1024)S(1)} %get-tuple-element.46) | copy-start | bytes 18436
  10.8 181.5 %copy-start.23 = (f32[1536]{0:T(1024)}, f32[1536]{0:T(1024)S(1)}, u32[]{:S(2)}) copy-start(f32[1536]{0:T(1024)S(1)} %get-tuple-element.47) | copy-start | bytes 18436
  10.8 181.5 %copy-start.24 = (f32[1536]{0:T(1024)}, f32[1536]{0:T(1024)S(1)}, u32[]{:S(2)}) copy-start(f32[1536]{0:T(1024)S(1)} %get-tuple-element.48) | copy-start | bytes 18436
  10.8 181.5 %copy-start.25 = (f32[1536]{0:T(1024)}, f32[1536]{0:T(1024)S(1)}, u32[]{:S(2)}) copy-start(f32[1536]{0:T(1024)S(1)} %get-tuple-element.49) | copy-start | bytes 18436
  10.8 181.5 %copy-start.26 = (f32[1536]{0:T(1024)}, f32[1536]{0:T(1024)S(1)}, u32[]{:S(2)}) copy-start(f32[1536]{0:T(1024)S(1)} %get-tuple-element.50) | copy-start | bytes 18436
  186.2 5.9 collective-permute-start.1
  187.7 4.5 collective-permute-start
  324.9 6.6 %collective-permute-start.3 = (f32[15,1536]{1,0:T(8,128)S(1)}, f32[15,1536]{1,0:T(8,128)S(1)}, u32[]{:S(2)}, u32[]{:S(2)}) collective-permute-start(f32[15,1536]{1,0:T(8,128)S(1)} %get-tuple-element.81), channel_id=1, source_target_pairs={{1,0},{2,1},{3,2},{4,3},{5,4},{6,5},{7,6},{9,8},{10,9},{11,10},{12... | collective-permute-start | bytes 276488 | tf_op jit(solution)/shard_map/ppermute | solution.py:19
  326.2 5.3 collective-permute-start.2
  358.4 28.2 %all-to-all-start = ((bf16[4,2,49152]{2,1,0:T(2,128)(2,1)}), bf16[4,2,49152]{2,1,0:T(2,128)(2,1)S(1)}, u32[]{:S(2)}, u32[]{:S(2)}) async-start(bf16[4,2,49152]{2,1,0:T(2,128)(2,1)} %reshape.100), calls=%async_computation | async-start | bytes 1572864 | tf_op jit(solution)/shard_map/all_to_all | solution.py:92
  361.9 142.4 %all-reduce.6.cloned.1.call-start = ((), (), s32[]{:S(2)}) async-start(), calls=%async_computation.4 | async-start | bytes 393216 | tf_op jit(solution)/shard_map/psum | solution.py:85
  368.1 227.6 %all-reduce.4.cloned.1.call-start = ((), (), s32[]{:S(2)}) async-start(), calls=%async_computation.3 | async-start | bytes 9437184 | tf_op jit(solution)/shard_map/psum | solution.py:99
  (26 other events, 503.1 us)
Sparse Core Ops, SparseCore 0:
  9.6 169.4 all-gather.2
  331.6 44.2 all-gather.4
  382.1 122.2 all-reduce.5
  508.1 87.5 all-reduce.3
where the time goes:
time: 609 us; the launch traced here: 608 us
  waiting for transfers between devices  384 us (63%)
  blocking collectives  121 us (20%)
  other arithmetic  39.5 us (6%)
  local copies, waits for them, and re-layouts  17.8 us (3%)
  matrix products  17.1 us (3%)
  between operations  15.4 us (3%)
  starting transfers between devices  12.8 us (2%)
    all_gather x1, waiting for transfers between devices, per_device(): weights = lax.all_gather(in_weight, 'dp', axis=0, tiled=True)  168 us
    psum x1, waiting for transfers between devices, per_device(): kernel_grad = lax.psum(kernel_part, ('dp', 'seq'))  105 us
    psum x1, waiting for transfers between devices, per_device(): weight_grad = lax.psum(local_rows, 'seq')  91.3 us
    psum x1, blocking collectives, per_device(): lax.psum(jnp.sum(centered * centered, axis=0), ('dp', 'seq')) / counted  42.5 us
    psum x1, blocking collectives, per_device(): lax.psum(jnp.sum(conv_out * valid_mask, axis=0), ('dp', 'seq')) / counted  40.2 us
    psum x1, blocking collectives, per_device(): lax.psum((jnp.sum(grad_shaped, axis=0), jnp.sum(grad_shaped * normed, axi...  38.3 us
    all_to_all x1, waiting for transfers between devices, per_device(): lax.all_to_all(grad_pre[None], 'dp', split_axis=2, concat_axis=0, tiled=T...  18.3 us
    unnamed x1, other arithmetic  17 us
  transfers between devices with their start and end apart: 9, of which 4 were waited for; matrix products, arithmetic and copies ran while one was open for 8% of the time, Pallas kernels for 0%

commit v1 on v0

--- a/solution.py
+++ b/solution.py
@@ -51,7 +51,8 @@
         :, None
     ]
     restored = restore(saved_codes[0], code_scales[0])
-    weights = lax.all_gather(in_weight, "dp", axis=0, tiled=True)
+    stack = jnp.stack([in_weight] * lax.axis_size("dp"))
+    weights = jnp.concatenate(lax.all_to_all(stack, "dp", 0, 0), axis=0)
     pre_act = lax.dot_general(
         restored, weights, (((1,), (1,)), ((), ())), preferred_element_type=jnp.float32
     )

time: 609 us -> 651 us (1.069)
  waiting for transfers between devices: 384 us -> 413 us
    all_to_all x0 -> x1, waiting for transfers between devices: none -> 204 us  [per_device(): weights = jnp.concatenate(lax.all_to_all(stack, 'dp', 0, 0), axis=0)]
    all_gather x1 -> x0, waiting for transfers between devices: 168 us -> none  [per_device(): weights = lax.all_gather(in_weight, 'dp', axis=0, tiled=True)]
  transfers between devices with their start and end apart: 9 -> 9, of which waited for: 4 -> 4; matrix products, arithmetic and copies ran while one was open for 8% -> 7% of each run, Pallas kernels for 0% -> 0%
where the time goes in v1:
time: 651 us; the launch traced here: 650 us
  waiting for transfers between devices  413 us (63%)
  blocking collectives  120 us (18%)
  other arithmetic  39.5 us (6%)
  local copies, waits for them, and re-layouts  23.7 us (4%)
  starting transfers between devices  19.3 us (3%)
  matrix products  17.1 us (3%)
  between operations  17.1 us (3%)
    all_to_all x1, waiting for transfers between devices, per_device(): weights = jnp.concatenate(lax.all_to_all(stack, 'dp', 0, 0), axis=0)  204 us
    psum x1, waiting for transfers between devices, per_device(): kernel_grad = lax.psum(kernel_part, ('dp', 'seq'))  99.9 us
    psum x1, waiting for transfers between devices, per_device(): weight_grad = lax.psum(local_rows, 'seq')  91 us
    psum x1, blocking collectives, per_device(): lax.psum(jnp.sum(centered * centered, axis=0), ('dp', 'seq')) / counted  42.3 us
    psum x1, blocking collectives, per_device(): lax.psum(jnp.sum(conv_out * valid_mask, axis=0), ('dp', 'seq')) / counted  39.4 us
    psum x1, blocking collectives, per_device(): lax.psum((jnp.sum(grad_shaped, axis=0), jnp.sum(grad_shaped * normed, axi...  38.6 us
    all_to_all x1, waiting for transfers between devices, per_device(): lax.all_to_all(grad_pre[None], 'dp', split_axis=2, concat_axis=0, tiled=T...  18.3 us
    unnamed x1, other arithmetic  17 us
  transfers between devices with their start and end apart: 9, of which 4 were waited for; matrix products, arithmetic and copies ran while one was open for 7% of the time, Pallas kernels for 0%

profile of v1, /device:TPU:0, one launch (start us, length us, event | category | flops | bytes accessed | tf_op | source)
XLA Modules:
  0.0 650.2 jit_solution(4459896051274196234)
XLA Ops:
  8.0 6.1 stack.103
  14.1 6.5 all-to-all-start
  23.2 204.1 %all-to-all-done = bf16[4,768,1536]{2,1,0:T(8,128)(2,1)} async-done(((bf16[4,768,1536]{2,1,0:T(8,128)(2,1)}), bf16[4,768,1536]{2,1,0:T(8,128)(2,1)}, u32[]{:S(2)}, u32[]{:S(2)}) %all-to-all-start) | async-done | bytes 9437216 | tf_op jit(solution)/shard_map/all_to_all | solution.py:55
  227.3 6.9 %fusion.197 = f32[128,3072]{1,0:T(8,128)S(1)} fusion(bf16[128,1536]{0,1:T(8,128)(2,1)S(1)} %bitcast.45, bf16[3072,1536]{1,0:T(8,128)(2,1)} %bitcast.3), kind=kOutput, calls=%fused_computation.396 | convolution fusion | flops 1207959552 | bytes 11403264 | tf_op jit(solution)/shard_map/dot_general | solution.py:56
  234.5 1.4 collective-permute-start.1
  235.9 3.0 collective-permute-start
  240.6 5.1 multiply_reduce_fusion.2
  245.6 39.4 %psum.42 = f32[1536]{0:T(1024)S(1)} all-reduce(f32[1536]{0:T(1024)S(1)} %get-tuple-element.78), channel_id=1, replica_groups=mesh['dp'=4,'seq'=8] {'dp','seq'}, use_global_device_ids=true, to_apply=%region_2.3 | all-reduce | flops 1536 | bytes 12288 | tf_op jit(solution)/shard_map/psum | solution.py:64
  285.2 42.3 %psum.43 = f32[1536]{0:T(1024)S(1)} all-reduce(f32[1536]{0:T(1024)S(1)} %multiply_reduce_fusion.1), channel_id=1, replica_groups=mesh['dp'=4,'seq'=8] {'dp','seq'}, use_global_device_ids=true, to_apply=%region_5.6 | all-reduce | flops 1536 | bytes 12288 | tf_op jit(solution)/shard_map/psum | solution.py:66
  327.5 1.3 fusion.193
  330.1 38.6 %all-reduce = (f32[1536]{0:T(1024)}, f32[1536]{0:T(1024)}) all-reduce(f32[1536]{0:T(1024)S(1)} %get-tuple-element.36, f32[1536]{0:T(1024)S(1)} %get-tuple-element.35), channel_id=1, replica_groups=mesh['dp'=4,'seq'=8] {'dp','seq'}, use_global_device_ids=true, to_apply=%region_9.10 | all-reduce | flops 3072 | bytes 24576 | tf_op jit(solution)/shard_map/psum | solution.py:74
  368.7 3.8 fusion.148
  373.8 3.2 collective-permute-start.2
  379.1 5.3 multiply_convert_fusion.1
  385.6 1.9 copy.22
  388.0 17.0 %reduce.62 = bf16[3072,128]{1,0:T(8,128)(2,1)S(1)} reduce(bf16[3072,1,128]{2,1,0:T(2,128)(2,1)S(1)} %bitcast.41, bf16[]{:T(256)} %broadcast.73), dimensions={1}, to_apply=%bitcast.32.reduce_sub_computation | reduce | bytes 1572866
  406.0 3.5 all-to-all-start.1
  412.8 2.8 stack.135
  415.9 18.3 %all-to-all-done.1 = bf16[4,2,49152]{2,1,0:T(2,128)(2,1)S(1)} async-done(((bf16[4,2,49152]{2,1,0:T(2,128)(2,1)}), bf16[4,2,49152]{2,1,0:T(2,128)(2,1)S(1)}, u32[]{:S(2)}, u32[]{:S(2)}) %all-to-all-start.1) | async-done | bytes 786464 | tf_op jit(solution)/shard_map/all_to_all | solution.py:93
  435.0 4.4 convolution_bitcast_fusion
  440.6 5.9 fusion
  446.4 99.9 %all-reduce.6.cloned.1.call-done = f32[31,1536]{1,0:T(8,128)} async-done(((f32[31,1536]{1,0:T(8,128)}), f32[31,1536]{1,0:T(8,128)}) %all-reduce.6.cloned.1.call-update) | async-done | bytes 190480 | tf_op jit(solution)/shard_map/psum | solution.py:86
  546.3 91.0 %all-reduce.4.cloned.1.call-done = f32[768,1536]{1,0:T(8,128)} async-done(((f32[768,1536]{1,0:T(8,128)}), f32[768,1536]{1,0:T(8,128)}) %all-reduce.4.cloned.1.call-update) | async-done | bytes 4718608 | tf_op jit(solution)/shard_map/psum | solution.py:100
  637.3 4.8 copy.30
  (150 shorter events, 16.8 us)
Async XLA Ops:
  14.1 213.3 %all-to-all-start = ((bf16[4,768,1536]{2,1,0:T(8,128)(2,1)}), bf16[4,768,1536]{2,1,0:T(8,128)(2,1)}, u32[]{:S(2)}, u32[]{:S(2)}) async-start(bf16[4,768,1536]{2,1,0:T(8,128)(2,1)} %stack.103), calls=%async_computation | async-start | bytes 18874368 | tf_op jit(solution)/shard_map/all_to_all | solution.py:55
  20.6 414.5 %all-gather.2.cloned.1.call-start = ((), (), s32[]{:S(2)}) async-start(), calls=%async_computation.2 | async-start | bytes 1966080 | tf_op jit(solution)/shard_map/all_gather | solution.py:96
  20.8 206.5 %copy-start = (bf16[1,128,1536]{1,2,0:T(8,128)(2,1)}, bf16[1,128,1536]{1,2,0:T(8,128)(2,1)S(1)}, u32[]{:S(2)}) copy-start(bf16[1,128,1536]{1,2,0:T(8,128)(2,1)S(1)} %copy.21) | copy-start | bytes 1179652
  22.1 212.1 %copy-start.37 = (f32[128]{0:T(128)}, f32[128]{0:T(128)S(1)}, u32[]{:S(2)}) copy-start(f32[128]{0:T(128)S(1)} %compare_convert_fusion) | copy-start | bytes 1540
  23.0 217.4 %copy-start.13 = (f32[1536]{0:T(1024)}, f32[1536]{0:T(1024)S(1)}, u32[]{:S(2)}) copy-start(f32[1536]{0:T(1024)S(1)} %get-tuple-element.38) | copy-start | bytes 18436
  23.0 217.4 %copy-start.15 = (f32[1536]{0:T(1024)}, f32[1536]{0:T(1024)S(1)}, u32[]{:S(2)}) copy-start(f32[1536]{0:T(1024)S(1)} %get-tuple-element.39) | copy-start | bytes 18436
  23.1 217.4 %copy-start.16 = (f32[1536]{0:T(1024)}, f32[1536]{0:T(1024)S(1)}, u32[]{:S(2)}) copy-start(f32[1536]{0:T(1024)S(1)} %get-tuple-element.40) | copy-start | bytes 18436
  23.1 217.4 %copy-start.17 = (f32[1536]{0:T(1024)}, f32[1536]{0:T(1024)S(1)}, u32[]{:S(2)}) copy-start(f32[1536]{0:T(1024)S(1)} %get-tuple-element.41) | copy-start | bytes 18436
  23.1 217.4 %copy-start.18 = (f32[1536]{0:T(1024)}, f32[1536]{0:T(1024)S(1)}, u32[]{:S(2)}) copy-start(f32[1536]{0:T(1024)S(1)} %get-tuple-element.42) | copy-start | bytes 18436
  23.1 217.4 %copy-start.19 = (f32[1536]{0:T(1024)}, f32[1536]{0:T(1024)S(1)}, u32[]{:S(2)}) copy-start(f32[1536]{0:T(1024)S(1)} %get-tuple-element.43) | copy-start | bytes 18436
  23.1 217.4 %copy-start.20 = (f32[1536]{0:T(1024)}, f32[1536]{0:T(1024)S(1)}, u32[]{:S(2)}) copy-start(f32[1536]{0:T(1024)S(1)} %get-tuple-element.44) | copy-start | bytes 18436
  23.1 217.4 %copy-start.21 = (f32[1536]{0:T(1024)}, f32[1536]{0:T(1024)S(1)}, u32[]{:S(2)}) copy-start(f32[1536]{0:T(1024)S(1)} %get-tuple-element.45) | copy-start | bytes 18436
  23.1 217.4 %copy-start.22 = (f32[1536]{0:T(1024)}, f32[1536]{0:T(1024)S(1)}, u32[]{:S(2)}) copy-start(f32[1536]{0:T(1024)S(1)} %get-tuple-element.46) | copy-start | bytes 18436
  23.1 217.4 %copy-start.23 = (f32[1536]{0:T(1024)}, f32[1536]{0:T(1024)S(1)}, u32[]{:S(2)}) copy-start(f32[1536]{0:T(1024)S(1)} %get-tuple-element.47) | copy-start | bytes 18436
  23.1 217.4 %copy-start.24 = (f32[1536]{0:T(1024)}, f32[1536]{0:T(1024)S(1)}, u32[]{:S(2)}) copy-start(f32[1536]{0:T(1024)S(1)} %get-tuple-element.48) | copy-start | bytes 18436
  23.1 217.4 %copy-start.25 = (f32[1536]{0:T(1024)}, f32[1536]{0:T(1024)S(1)}, u32[]{:S(2)}) copy-start(f32[1536]{0:T(1024)S(1)} %get-tuple-element.49) | copy-start | bytes 18436
  23.1 217.4 %copy-start.26 = (f32[1536]{0:T(1024)}, f32[1536]{0:T(1024)S(1)}, u32[]{:S(2)}) copy-start(f32[1536]{0:T(1024)S(1)} %get-tuple-element.50) | copy-start | bytes 18436
  234.5 5.9 collective-permute-start.1
  235.9 4.5 collective-permute-start
  372.5 6.6 %collective-permute-start.3 = (f32[15,1536]{1,0:T(8,128)S(1)}, f32[15,1536]{1,0:T(8,128)S(1)}, u32[]{:S(2)}, u32[]{:S(2)}) collective-permute-start(f32[15,1536]{1,0:T(8,128)S(1)} %get-tuple-element.81), channel_id=1, source_target_pairs={{1,0},{2,1},{3,2},{4,3},{5,4},{6,5},{7,6},{9,8},{10,9},{11,10},{12... | collective-permute-start | bytes 276488 | tf_op jit(solution)/shard_map/ppermute | solution.py:19
  373.8 5.3 collective-permute-start.2
  406.0 28.2 %all-to-all-start.1 = ((bf16[4,2,49152]{2,1,0:T(2,128)(2,1)}), bf16[4,2,49152]{2,1,0:T(2,128)(2,1)S(1)}, u32[]{:S(2)}, u32[]{:S(2)}) async-start(bf16[4,2,49152]{2,1,0:T(2,128)(2,1)} %reshape.117), calls=%async_computation.1 | async-start | bytes 1572864 | tf_op jit(solution)/shard_map/all_to_all | solution.py:93
  409.5 136.8 %all-reduce.6.cloned.1.call-start = ((), (), s32[]{:S(2)}) async-start(), calls=%async_computation.4 | async-start | bytes 393216 | tf_op jit(solution)/shard_map/psum | solution.py:86
  415.6 221.7 %all-reduce.4.cloned.1.call-start = ((), (), s32[]{:S(2)}) async-start(), calls=%async_computation.3 | async-start | bytes 9437184 | tf_op jit(solution)/shard_map/psum | solution.py:100
  (26 other events, 521.0 us)
Sparse Core Ops, SparseCore 0:
  379.2 43.8 all-gather.1
Sparse Core Ops, SparseCore 1:
  416.1 130.2 all-reduce.5
  550.1 87.1 all-reduce.3
